TPU v7x, 32 devices: a whole 2x2x4 slice. The times are simulated.
32 devices in a mesh: tm: 8 (over z, core), space: 4 (over y, x).
Axes of the slice: x: 2, y: 2, z: 4, core: 2. Of those that a mesh axis runs over, the one named last changes fastest.
Arguments:
- solution: float32 [512, 384, 384], P('tm', 'space'), may hold values from -6 to 6
- residual: float32 [512, 384, 384], P('tm', 'space'), may hold values from -6 to 6
- direction: float32 [512, 384, 384], P('tm', 'space'), may hold values from -6 to 6
- reaction: float32 [512, 384, 384], P('tm', 'space'), may hold values from 0.1 to 2
- time_bands: float32 [2, 4, 512], replicated, may hold values from -0.25 to 1.1, as said below
- space_bands: float32 [2, 4, 384], replicated, may hold values from -0.25 to 1.1, as said below
- time_basis: float32 [512, 512], replicated, may hold values from -0.25 to 0.25
- space_basis: float32 [384, 384], replicated, may hold values from -0.3125 to 0.3125
- time_eigen: float32 [512], replicated, may hold values from 0.1 to 1
- space_eigen: float32 [384], replicated, may hold values from 0.1 to 1
Outputs:
- new_solution: float32 [512, 384, 384], P('tm', 'space')
- new_residual: float32 [512, 384, 384], P('tm', 'space')
- new_direction: float32 [512, 384, 384], P('tm', 'space')
Inputs may be any that keep to these rules, and one draw needn't show every extreme that they name: `time_bands`: each of the two matrices is symmetric with every diagonal entry larger than the sum of the magnitudes of the other entries of its row. `space_bands`: each of the two matrices is symmetric with every diagonal entry larger than the sum of the magnitudes of the other entries of its row.
All inputs are finite; a program needn't handle non-finite values.
Results may differ from a plain program's by a relative error of at most 0.000051.
Values sent between devices are 32-bit elements; how exact they have to be, the bound alone decides.
No kernel may reach another device: no remote copies, remote signals or barrier semaphores. Data moves between devices by JAX's collectives and lax.ppermute only.
A program may use at most 192 MiB of HBM per device.

v0:
```python
import jax
import jax.numpy as jnp
from jax import lax
from jax.sharding import PartitionSpec as P

highest = lax.Precision.HIGHEST


def extended_2(cells, sides, width):
    for axis, dim in sides:
        count = lax.axis_size(axis)
        ends = count - 1
        head = lax.slice_in_dim(cells, 0, width, axis=dim)
        tail = lax.slice_in_dim(cells, cells.shape[dim] - width, cells.shape[dim], axis=dim)
        cells = jnp.concatenate(
            [
                lax.ppermute(tail, axis, [(i, (i + 1) % count) for i in range(ends)]),
                cells,
                lax.ppermute(head, axis, [((i + 1) % count, i) for i in range(ends)]),
            ],
            axis=dim,
        )
    return cells


def band_apply(extended, band_rows, dimension):
    length = extended.shape[dimension] - 6
    target_shape = [1] * extended.ndim
    target_shape[dimension] = length

    def coefficient(which_row, first_row):
        return lax.slice_in_dim(band_rows[which_row], first_row, first_row + length).reshape(
            target_shape
        )

    def window(first_row):
        return lax.slice_in_dim(extended, first_row, first_row + length, axis=dimension)

    result = coefficient(0, 3) * window(3)
    for offset in (1, 2, 3):
        result = (
            result
            + coefficient(offset, 3) * window(3 + offset)
            + coefficient(offset, 3 - offset) * window(3 - offset)
        )
    return result


def pad_along(values, dimension):
    widths = [(0, 0)] * values.ndim
    widths[dimension] = (3, 3)
    return jnp.pad(values, widths)


def apply_operator(direction, reaction, time_bands, space_bands):
    rows_time = direction.shape[0]
    rows_space = direction.shape[1]
    halo_block = extended_2(direction, (("tm", 0), ("space", 1)), 3)
    padded_time = jnp.pad(time_bands, ((0, 0), (0, 0), (3, 3)))
    padded_space = jnp.pad(space_bands, ((0, 0), (0, 0), (3, 3)))
    time_rows = lax.dynamic_slice_in_dim(
        padded_time, lax.axis_index("tm") * rows_time, rows_time + 6, 2
    )
    space_rows = lax.dynamic_slice_in_dim(
        padded_space, lax.axis_index("space") * rows_space, rows_space + 6, 2
    )
    extended = pad_along(halo_block, 2)
    mass_y = band_apply(extended, padded_space[1], 2)
    stiff_y = band_apply(extended, padded_space[0], 2)
    mass_xy = band_apply(mass_y, space_rows[1], 1)
    stiff_x = band_apply(mass_y, space_rows[0], 1)
    stiff_yx = band_apply(stiff_y, space_rows[1], 1)
    temporal = band_apply(mass_xy, time_rows[0], 0) + band_apply(
        stiff_x + stiff_yx, time_rows[1], 0
    )
    return temporal + reaction * direction


def spectrum(time_eigen, space_eigen):
    time_count = lax.axis_size("tm")
    space_count = lax.axis_size("space")
    block_width = space_eigen.shape[0] // (time_count * space_count)
    group_index = lax.axis_index("space") * time_count + lax.axis_index("tm")
    block = lax.dynamic_slice_in_dim(space_eigen, group_index * block_width, block_width)
    return time_eigen[:, None, None] + space_eigen[None, :, None] + block[None, None, :]


def forward_fields(fields, time_basis, space_basis):
    along_y = jnp.einsum("ctxk,ka->ctxa", fields, space_basis, precision=highest)
    spread = lax.all_to_all(along_y, "space", split_axis=3, concat_axis=2, tiled=True)
    along_x = jnp.einsum("ctjy,jb->ctby", spread, space_basis, precision=highest)
    joined = lax.all_to_all(along_x, "tm", split_axis=3, concat_axis=1, tiled=True)
    return jnp.einsum("cixy,ia->caxy", joined, time_basis, precision=highest)


def inverse_fields(spectral, time_basis, space_basis):
    along_t = jnp.einsum("caxy,ia->cixy", spectral, time_basis, precision=highest)
    parted = lax.all_to_all(along_t, "tm", split_axis=1, concat_axis=3, tiled=True)
    along_x = jnp.einsum("ctby,jb->ctjy", parted, space_basis, precision=highest)
    blocks = lax.all_to_all(along_x, "space", split_axis=2, concat_axis=3, tiled=True)
    return jnp.einsum("ctxa,ka->ctxk", blocks, space_basis, precision=highest)


def per_device(
    solution,
    residual,
    direction,
    reaction,
    time_bands,
    space_bands,
    time_basis,
    space_basis,
    time_eigen,
    space_eigen,
):
    image = apply_operator(direction, reaction, time_bands, space_bands)
    eigen_sum = spectrum(time_eigen, space_eigen)
    both_hat = forward_fields(jnp.stack([residual, image]), time_basis, space_basis)
    first_scaled = both_hat[0] / eigen_sum
    image_scaled = both_hat[1] / eigen_sum
    norm_old, cross_term, image_norm, curvature = lax.psum(
        (
            jnp.sum(both_hat[0] * first_scaled),
            jnp.sum(both_hat[1] * first_scaled),
            jnp.sum(both_hat[1] * image_scaled),
            jnp.sum(direction * image),
        ),
        ("tm", "space"),
    )
    step_size = norm_old / curvature
    new_residual = residual - step_size * image
    spectral = first_scaled - step_size * image_scaled
    norm_new = norm_old - 2.0 * step_size * cross_term + step_size * step_size * image_norm
    precond = inverse_fields(spectral[None], time_basis, space_basis)[0]
    new_direction = precond + norm_new / norm_old * direction
    new_solution = solution + step_size * direction
    return (new_solution, new_residual, new_direction)


def solution(mesh):
    return jax.shard_map(
        per_device,
        mesh=mesh,
        in_specs=(
            P("tm", "space", None),
            P("tm", "space", None),
            P("tm", "space", None),
            P("tm", "space", None),
            P(),
            P(),
            P(),
            P(),
            P(),
            P(),
        ),
        out_specs=(P("tm", "space", None), P("tm", "space", None), P("tm", "space", None)),
        check_vma=False,
    )
```

profile of v0, /device:TPU:0, one launch (start us, length us, event | category | flops | bytes accessed | tf_op | source)
XLA Modules:
  0.0 1760.0 jit_solution(4880386826261498902)
XLA Ops:
  0.6 0.0 copy-start
  0.6 1.3 fusion.90
  1.9 2.4 collective-permute-start
  4.4 1.3 collective-permute-start.1
  5.7 0.9 fusion.72
  6.5 1.0 fusion.71
  7.6 0.0 collective-permute-done
  7.6 0.0 copy-start.4
  7.7 0.0 copy-start.3
  7.7 4.9 constant_dynamic-update-slice_fusion.1
  12.6 0.0 collective-permute-done.1
  12.6 0.2 fusion.89
  12.8 4.2 collective-permute-start.2
  17.0 1.3 collective-permute-start.3
  18.3 0.0 copy-done.4
  18.4 0.1 fusion.61
  18.4 0.1 fusion.59
  18.6 0.0 copy-done.3
  18.6 0.1 slice_reduce_fusion.7
  18.7 5.7 collective-permute-done.2
  24.4 11.1 collective-permute-done.3
  35.6 5.1 pad_maximum_fusion
  40.7 85.2 %multiply_add_fusion.1 = (f32[70,102,384]{2,1,0:T(8,128)}, f32[70,102,384]{2,1,0:T(8,128)}) fusion(f32[70,102,384]{2,1,0:T(8,128)} %pad_maximum_fusion, f32[384]{0:T(512)S(1)} %get-tuple-element.9, f32[384]{0:T(512)S(1)} %get-tuple-element.15, f32[384]{0:T(512)S(1)} %get-tuple-element.8, f32[384]{0:T(512)S(1)} %get-tuple-element.16, ...), kind=kLoop, calls=%fused_computation.18 | loop fusion | flops 71285760 | bytes 32922624 | tf_op jit(solution)/shard_map/add | solution.py:42
  125.9 31.0 %multiply_add_fusion.2 = f32[70,96,384]{2,1,0:T(8,128)} fusion(f32[70,102,384]{2,1,0:T(8,128)} %get-tuple-element.26, f32[96]{0:T(128)S(1)} %get-tuple-element.54, f32[96]{0:T(128)S(1)} %get-tuple-element.55, f32[96]{0:T(128)S(1)} %get-tuple-element.56, f32[96]{0:T(128)S(1)} %get-tuple-element.57, f32[96]{0:T(128)S(1)} %get-tuple-element.59, ...), kind=kLoop, calls=%fused_computation.33 | loop fusion | flops 33546240 | bytes 82578048 | tf_op jit(solution)/shard_map/add | solution.py:42
  156.9 56.5 %fusion.5 = f32[70,96,384]{2,1,0:T(8,128)} fusion(f32[70,102,384]{2,1,0:T(8,128)} %get-tuple-element.27, f32[70,102,384]{2,1,0:T(8,128)} %get-tuple-element.26, f32[96]{0:T(128)S(1)} %get-tuple-element.48, f32[96]{0:T(128)S(1)} %get-tuple-element.49, f32[96]{0:T(128)S(1)} %get-tuple-element.47, f32[96]{0:T(128)S(1)} %get-tuple-element.50, ...), kind=kLoop, calls=%fused_computation.21 | loop fusion | flops 69672960 | bytes 154834176 | tf_op jit(solution)/shard_map/add | solution.py:74
  213.5 0.0 copy-start.2
  213.5 55.2 %multiply_reduce_fusion = (f32[]{:T(128)}, f32[64,96,384]{2,1,0:T(8,128)}) fusion(f32[64,96,384]{2,1,0:T(8,128)} %param.12, f32[64,96,384]{2,1,0:T(8,128)} %param.13, f32[70,96,384]{2,1,0:T(8,128)} %fusion.5, f32[64]{0:T(128)S(1)} %get-tuple-element.38, f32[64]{0:T(128)S(1)} %get-tuple-element.39, f32[64]{0:T(128)S(1)} %get-tuple-element.37, ...), kind=kLoop, calls=%fused_computation.75 | loop fusion | flops 73138176 | bytes 160435712 | tf_op jit(solution)/shard_map/reduce_sum | solution.py:126
  268.7 0.0 copy-done.2
  268.7 40.4 %fusion = f32[2,64,96,384]{3,2,1,0:T(8,128)} fusion(f32[1,64,96,384]{3,2,1,0:T(8,128)} %bitcast.137, f32[1,64,96,384]{3,2,1,0:T(8,128)} %bitcast.141, f32[384,384]{1,0:T(8,128)S(1)} %copy-done.2), kind=kOutput, calls=%fused_computation.7 | convolution fusion | flops 21747990528 | bytes 38338560 | tf_op jit(solution)/shard_map/ctxk,ka->ctxa/dot_general | solution.py:89
  309.1 22.2 %copy.37 = f32[2,64,96,384]{2,1,0,3:T(8,128)} copy(f32[2,64,96,384]{3,2,1,0:T(8,128)} %fusion) | data formatting | bytes 37748736 | tf_op jit(solution)/shard_map/ctxk,ka->ctxa/dot_general | solution.py:89
  331.3 288.6 %all_to_all.66 = f32[2,64,96,384]{2,1,0,3:T(8,128)S(1)} all-to-all(f32[2,64,96,384]{2,1,0,3:T(8,128)} %copy.37), channel_id=1, replica_groups=mesh['tm'=8,'space'=4] {'space'}, dimensions={3} | all-to-all | bytes 37748736 | tf_op jit(solution)/shard_map/all_to_all | solution.py:90
  619.9 36.2 %copy.59 = f32[2,64,96,4,96]{2,3,4,1,0:T(4,128)} copy(f32[2,64,96,4,96]{2,1,0,4,3:T(8,128)S(1)} %bitcast.135) | data formatting | bytes 37748736 | tf_op jit(solution)/shard_map/all_to_all | solution.py:90
  656.2 26.3 %all_to_all.51 = f32[2,64,384,96]{2,3,1,0:T(8,128)} reshape(f32[2,64,4,96,96]{3,2,4,1,0:T(4,128)} %bitcast.136) | data formatting | bytes 37748736 | tf_op jit(solution)/shard_map/all_to_all | solution.py:90
  682.4 43.2 %convolution_bitcast_fusion.1 = f32[2,64,384,96]{2,3,1,0:T(8,128)S(1)} fusion(f32[2,64,384,96]{2,3,1,0:T(8,128)} %all_to_all.51, f32[384,384]{1,0:T(8,128)S(1)} %copy-done.2), kind=kOutput, calls=%fused_computation.80 | convolution fusion | flops 21743271936 | bytes 38338560 | tf_op jit(solution)/shard_map/ctjy,jb->ctby/dot_general | solution.py:91
  725.6 21.8 %copy.39 = f32[2,64,384,96]{2,1,0,3:T(8,128)} copy(f32[2,64,384,96]{2,3,1,0:T(8,128)S(1)} %convolution_bitcast_fusion.1) | data formatting | bytes 37748736 | tf_op jit(solution)/shard_map/ctjy,jb->ctby/transpose | solution.py:91
  747.4 0.0 copy-start.5
  747.5 0.0 copy-start.6
  747.5 9.2 all-to-all-start.1
  756.6 0.0 copy-done.5
  756.6 0.1 dynamic_slice.11
  756.7 0.0 copy-done.6
  756.7 0.1 broadcast_add_fusion
  756.8 408.5 %all-to-all-done.1 = f32[2,64,384,96]{2,1,0,3:T(8,128)} async-done(((f32[2,64,384,96]{2,1,0,3:T(8,128)}), f32[2,64,384,96]{2,1,0,3:T(8,128)}, u32[]{:S(2)}, u32[]{:S(2)}) %all-to-all-start.1) | async-done | bytes 18874400 | tf_op jit(solution)/shard_map/all_to_all | solution.py:92
  1165.3 12.9 copy.41
  1178.2 0.0 copy-done
  1178.2 35.3 %convolution_bitcast_fusion = f32[2,512,384,12]{1,2,3,0:T(8,128)S(1)} fusion(f32[2,512,384,12]{2,1,3,0:T(8,128)} %bitcast.134, f32[512,512]{1,0:T(8,128)S(1)} %copy-done), kind=kOutput, calls=%fused_computation.79 | convolution fusion | flops 28991029248 | bytes 38797312 | tf_op jit(solution)/shard_map/cixy,ia->caxy/dot_general | solution.py:93
  1213.5 0.0 copy-start.1
  1213.5 6.5 copy-done.1
  1219.9 4.4 fusion.35
  1224.3 37.2 %all-reduce.3 = (f32[]{:T(128)}, f32[]{:T(128)}, f32[]{:T(128)}, f32[]{:T(128)}) all-reduce(f32[]{:T(128)} %get-tuple-element.5, f32[]{:T(128)} %get-tuple-element.24, f32[]{:T(128)} %get-tuple-element.4, f32[]{:T(128)} %get-tuple-element.3), channel_id=1, replica_groups=mesh['tm'=8,'space'=4] {'tm','space'}, use_global_device_ids=true, to_apply=%region_1.2 | all-reduce | flops 4 | bytes 32 | tf_op jit(solution)/shard_map/psum | solution.py:121
  1262.8 21.6 %fusion.44 = f32[1,512,384,12]{1,2,3,0:T(8,128)} fusion(f32[2,512,384,12]{1,2,3,0:T(8,128)} %copy-done.1, f32[]{:T(128)S(6)} %div.19, f32[12]{0:T(128)S(1)} %dynamic_slice.11, f32[512,384]{0,1:T(8,128)S(1)} %broadcast_add_fusion, f32[512,512]{1,0:T(8,128)S(1)} %copy-done), kind=kOutput, calls=%fused_computation.85 | convolution fusion | flops 14507311104 | bytes 30146612 | tf_op jit(solution)/shard_map/caxy,ia->cixy/dot_general | solution.py:97
  1284.4 23.1 %copy.43 = f32[1,512,384,12]{2,0,3,1:T(1,128)} copy(f32[1,512,384,12]{1,2,3,0:T(8,128)} %fusion.44) | data formatting | bytes 18874368 | tf_op jit(solution)/shard_map/caxy,ia->cixy/transpose | solution.py:97
  1307.5 210.6 %all_to_all.67 = f32[1,512,384,12]{2,0,3,1:T(1,128)S(1)} all-to-all(f32[1,512,384,12]{2,0,3,1:T(1,128)} %copy.43), channel_id=1, replica_groups=mesh['tm'=8,'space'=4] {'tm'}, dimensions={1} | all-to-all | bytes 18874368 | tf_op jit(solution)/shard_map/all_to_all | solution.py:98
  1518.1 4.6 copy.44
  1522.6 4.3 copy.45
  1527.0 24.3 %fusion.41 = f32[1,64,384,96]{2,3,1,0:T(8,128)} fusion(f32[64,384,96]{1,0,2:T(8,128)S(1)} %bitcast.138, f32[384,384]{1,0:T(8,128)S(1)} %copy-done.2), kind=kOutput, calls=%fused_computation.84 | convolution fusion | flops 10871635968 | bytes 19464192 | tf_op jit(solution)/shard_map/ctby,jb->ctjy/dot_general | solution.py:99
  1551.3 11.6 copy.47
  1562.9 6.6 all-to-all-start.3
  1572.0 12.0 multiply_subtract_fusion
  1584.0 12.0 multiply_add_fusion.4
  1596.0 111.5 %all-to-all-done.3 = f32[1,64,384,96]{3,1,0,2:T(8,128)} async-done(((f32[1,64,384,96]{3,1,0,2:T(8,128)}), f32[1,64,384,96]{3,1,0,2:T(8,128)}, u32[]{:S(2)}, u32[]{:S(2)}) %all-to-all-start.3) | async-done | bytes 9437216 | tf_op jit(solution)/shard_map/all_to_all | solution.py:100
  1707.4 16.4 copy.60
  1723.8 13.8 reshape.269
  1737.7 21.9 %multiply_add_fusion.3 = f32[64,96,384]{2,1,0:T(8,128)} fusion(f32[64,96,384]{2,1,0:T(8,128)} %param.12, f32[]{:T(128)S(6)} %div.23, f32[64,96,384]{2,1,0:T(8,128)} %reshape.269, f32[384,384]{1,0:T(8,128)S(1)} %copy-done.2), kind=kOutput, calls=%fused_computation.72 | convolution fusion | flops 10876354560 | bytes 28901380 | tf_op jit(solution)/shard_map/ctxa,ka->ctxk/dot_general | solution.py:101
  (2 shorter events, 0.1 us)
Async XLA Ops:
  0.6 1177.5 %copy-start = (f32[512,512]{1,0:T(8,128)S(1)}, f32[512,512]{1,0:T(8,128)}, u32[]{:S(2)}) copy-start(f32[512,512]{1,0:T(8,128)} %param.16) | copy-start | bytes 3145732
  1.9 5.7 collective-permute-start
  4.4 8.2 collective-permute-start.1
  7.6 10.7 copy-start.4
  7.7 10.9 copy-start.3
  12.8 11.6 collective-permute-start.2
  17.0 18.5 %collective-permute-start.3 = (f32[70,3,384]{2,1,0:T(4,128)S(1)}, f32[70,3,384]{2,1,0:T(4,128)S(1)}, u32[]{:S(2)}, u32[]{:S(2)}) collective-permute-start(f32[70,3,384]{2,1,0:T(4,128)S(1)} %get-tuple-element.29), channel_id=1, source_target_pairs={{1,0},{2,1},{3,2},{5,4},{6,5},{7,6},{9,8},{10,9},{11,10},{13,12},{... | collective-permute-start | bytes 967688 | tf_op jit(solution)/shard_map/ppermute | solution.py:19
  213.5 55.2 %copy-start.2 = (f32[384,384]{1,0:T(8,128)S(1)}, f32[384,384]{1,0:T(8,128)}, u32[]{:S(2)}) copy-start(f32[384,384]{1,0:T(8,128)} %param.17) | copy-start | bytes 1769476
  747.4 9.2 copy-start.5
  747.5 9.3 copy-start.6
  747.5 417.8 %all-to-all-start.1 = ((f32[2,64,384,96]{2,1,0,3:T(8,128)}), f32[2,64,384,96]{2,1,0,3:T(8,128)}, u32[]{:S(2)}, u32[]{:S(2)}) async-start(f32[2,64,384,96]{2,1,0,3:T(8,128)} %copy.39), calls=%async_computation.1 | async-start | bytes 37748736 | tf_op jit(solution)/shard_map/all_to_all | solution.py:92
  1213.5 6.5 copy-start.1
  1562.9 144.5 %all-to-all-start.3 = ((f32[1,64,384,96]{3,1,0,2:T(8,128)}), f32[1,64,384,96]{3,1,0,2:T(8,128)}, u32[]{:S(2)}, u32[]{:S(2)}) async-start(f32[1,64,384,96]{3,1,0,2:T(8,128)} %copy.47), calls=%async_computation.3 | async-start | bytes 25165824 | tf_op jit(solution)/shard_map/all_to_all | solution.py:100
where the time goes:
time: 1770 us; the launch traced here: 1760 us
  waiting for transfers between devices  537 us (30%)
  blocking collectives  536 us (30%)
  other arithmetic  262 us (15%)
  local copies, waits for them, and re-layouts  208 us (12%)
  matrix products  187 us (11%)
  starting transfers between devices  25 us (1%)
    all_to_all x1, waiting for transfers between devices, forward_fields(): lax.all_to_all(along_x, 'tm', split_axis=3, concat_axis=1, tiled=True)  408 us
    all_to_all x1, blocking collectives, forward_fields(): lax.all_to_all(along_y, 'space', split_axis=3, concat_axis=2, tiled=True)  289 us
    all_to_all x1, blocking collectives, inverse_fields(): lax.all_to_all(along_t, 'tm', split_axis=1, concat_axis=3, tiled=True)  211 us
    add x2, other arithmetic, band_apply(): result + coefficient(offset, 3) * window(3 + offset)  116 us
    all_to_all x1, waiting for transfers between devices, inverse_fields(): lax.all_to_all(along_x, 'space', split_axis=2, concat_axis=3, tiled=True)  111 us
    all_to_all x2, local copies, waits for them, and re-layouts, forward_fields(): lax.all_to_all(along_y, 'space', split_axis=3, concat_axis=2, tiled=True)  62.5 us
    add x1, other arithmetic, apply_operator(): stiff_x + stiff_yx  56.5 us
    reduce_sum x1, other arithmetic, per_device(): jnp.sum(direction * image)  55.2 us
  transfers between devices with their start and end apart: 6, of which 4 were waited for; matrix products, arithmetic and copies ran while one was open for 2% of the time, Pallas kernels for 0%

commit v1 on v0

--- a/solution.py
+++ b/solution.py
@@ -89,7 +89,10 @@
     along_y = jnp.einsum("ctxk,ka->ctxa", fields, space_basis, precision=highest)
     spread = lax.all_to_all(along_y, "space", split_axis=3, concat_axis=2, tiled=True)
     along_x = jnp.einsum("ctjy,jb->ctby", spread, space_basis, precision=highest)
-    joined = lax.all_to_all(along_x, "tm", split_axis=3, concat_axis=1, tiled=True)
+    joined = jnp.concatenate(
+        lax.all_to_all(jnp.stack(jnp.split(along_x, lax.axis_size("tm"), axis=3)), "tm", 0, 0),
+        axis=1,
+    )
     return jnp.einsum("cixy,ia->caxy", joined, time_basis, precision=highest)
 
 

time: 1770 us -> 1790 us (1.011)
    transpose x1 -> x0, local copies, waits for them, and re-layouts: 21.8 us -> none  [forward_fields(): jnp.einsum('ctjy,jb->ctby', spread, space_basis, precision=highest)]
    another operation x1 -> x3, local copies, waits for them, and re-layouts: 13.8 us -> 34.3 us  [the longest x2 20.4 us: forward_fields(): jnp.stack(jnp.split(along_x, lax.axis_size('tm'), axis=3))]
where the time goes in v1:
time: 1790 us; the launch traced here: 1770 us
  waiting for transfers between devices  537 us (30%)
  blocking collectives  536 us (30%)
  other arithmetic  262 us (15%)
  local copies, waits for them, and re-layouts  221 us (12%)
  matrix products  187 us (10%)
  starting transfers between devices  25 us (1%)
    all_to_all x1, waiting for transfers between devices, forward_fields(): lax.all_to_all(jnp.stack(jnp.split(along_x, lax.axis_size('tm'), axis=3))...  408 us
    all_to_all x1, blocking collectives, forward_fields(): lax.all_to_all(along_y, 'space', split_axis=3, concat_axis=2, tiled=True)  289 us
    all_to_all x1, blocking collectives, inverse_fields(): lax.all_to_all(along_t, 'tm', split_axis=1, concat_axis=3, tiled=True)  211 us
    add x2, other arithmetic, band_apply(): result + coefficient(offset, 3) * window(3 + offset)  116 us
    all_to_all x1, waiting for transfers between devices, inverse_fields(): lax.all_to_all(along_x, 'space', split_axis=2, concat_axis=3, tiled=True)  111 us
    all_to_all x2, local copies, waits for them, and re-layouts, forward_fields(): lax.all_to_all(along_y, 'space', split_axis=3, concat_axis=2, tiled=True)  62.5 us
    add x1, other arithmetic, apply_operator(): stiff_x + stiff_yx  56.5 us
    reduce_sum x1, other arithmetic, per_device(): jnp.sum(direction * image)  55.2 us
  transfers between devices with their start and end apart: 6, of which 4 were waited for; matrix products, arithmetic and copies ran while one was open for 2% of the time, Pallas kernels for 0%

profile of v1, /device:TPU:0, one launch (start us, length us, event | category | flops | bytes accessed | tf_op | source)
XLA Modules:
  0.0 1772.5 jit_solution(14855101598387709146)
XLA Ops:
  0.6 0.0 copy-start
  0.6 1.3 fusion.98
  1.9 2.4 collective-permute-start
  4.4 1.3 collective-permute-start.1
  5.7 0.9 fusion.80
  6.5 1.0 fusion.79
  7.6 0.0 collective-permute-done
  7.6 0.0 copy-start.4
  7.7 0.0 copy-start.3
  7.7 4.9 constant_dynamic-update-slice_fusion.1
  12.6 0.0 collective-permute-done.1
  12.6 0.2 fusion.97
  12.8 4.2 collective-permute-start.2
  17.0 1.3 collective-permute-start.3
  18.4 0.1 fusion.69
  18.4 0.1 fusion.67
  18.6 0.1 slice_reduce_fusion.7
  18.7 5.7 collective-permute-done.2
  24.4 11.1 collective-permute-done.3
  35.6 5.1 pad_maximum_fusion
  40.7 85.2 %multiply_add_fusion.1 = (f32[70,102,384]{2,1,0:T(8,128)}, f32[70,102,384]{2,1,0:T(8,128)}) fusion(f32[70,102,384]{2,1,0:T(8,128)} %pad_maximum_fusion, f32[384]{0:T(512)S(1)} %get-tuple-element.9, f32[384]{0:T(512)S(1)} %get-tuple-element.15, f32[384]{0:T(512)S(1)} %get-tuple-element.8, f32[384]{0:T(512)S(1)} %get-tuple-element.16, ...), kind=kLoop, calls=%fused_computation.18 | loop fusion | flops 71285760 | bytes 32922624 | tf_op jit(solution)/shard_map/add | solution.py:42
  125.9 31.0 %multiply_add_fusion.2 = f32[70,96,384]{2,1,0:T(8,128)} fusion(f32[70,102,384]{2,1,0:T(8,128)} %get-tuple-element.26, f32[96]{0:T(128)S(1)} %get-tuple-element.54, f32[96]{0:T(128)S(1)} %get-tuple-element.55, f32[96]{0:T(128)S(1)} %get-tuple-element.56, f32[96]{0:T(128)S(1)} %get-tuple-element.57, f32[96]{0:T(128)S(1)} %get-tuple-element.59, ...), kind=kLoop, calls=%fused_computation.33 | loop fusion | flops 33546240 | bytes 82578048 | tf_op jit(solution)/shard_map/add | solution.py:42
  156.9 56.5 %fusion.5 = f32[70,96,384]{2,1,0:T(8,128)} fusion(f32[70,102,384]{2,1,0:T(8,128)} %get-tuple-element.27, f32[70,102,384]{2,1,0:T(8,128)} %get-tuple-element.26, f32[96]{0:T(128)S(1)} %get-tuple-element.48, f32[96]{0:T(128)S(1)} %get-tuple-element.49, f32[96]{0:T(128)S(1)} %get-tuple-element.47, f32[96]{0:T(128)S(1)} %get-tuple-element.50, ...), kind=kLoop, calls=%fused_computation.21 | loop fusion | flops 69672960 | bytes 154834176 | tf_op jit(solution)/shard_map/add | solution.py:74
  213.5 0.0 copy-start.2
  213.5 55.2 %multiply_reduce_fusion = (f32[]{:T(128)}, f32[64,96,384]{2,1,0:T(8,128)}) fusion(f32[64,96,384]{2,1,0:T(8,128)} %param.12, f32[64,96,384]{2,1,0:T(8,128)} %param.13, f32[70,96,384]{2,1,0:T(8,128)} %fusion.5, f32[64]{0:T(128)S(1)} %get-tuple-element.38, f32[64]{0:T(128)S(1)} %get-tuple-element.39, f32[64]{0:T(128)S(1)} %get-tuple-element.37, ...), kind=kLoop, calls=%fused_computation.75 | loop fusion | flops 73138176 | bytes 160435712 | tf_op jit(solution)/shard_map/reduce_sum | solution.py:129
  268.7 40.4 %fusion = f32[2,64,96,384]{3,2,1,0:T(8,128)} fusion(f32[1,64,96,384]{3,2,1,0:T(8,128)} %bitcast.168, f32[1,64,96,384]{3,2,1,0:T(8,128)} %bitcast.172, f32[384,384]{1,0:T(8,128)S(1)} %copy-done.2), kind=kOutput, calls=%fused_computation.7 | convolution fusion | flops 21747990528 | bytes 38338560 | tf_op jit(solution)/shard_map/ctxk,ka->ctxa/dot_general | solution.py:89
  309.1 22.2 %copy.34 = f32[2,64,96,384]{2,1,0,3:T(8,128)} copy(f32[2,64,96,384]{3,2,1,0:T(8,128)} %fusion) | data formatting | bytes 37748736 | tf_op jit(solution)/shard_map/ctxk,ka->ctxa/dot_general | solution.py:89
  331.3 288.6 %all_to_all.53 = f32[2,64,96,384]{2,1,0,3:T(8,128)S(1)} all-to-all(f32[2,64,96,384]{2,1,0,3:T(8,128)} %copy.34), channel_id=1, replica_groups=mesh['tm'=8,'space'=4] {'space'}, dimensions={3} | all-to-all | bytes 37748736 | tf_op jit(solution)/shard_map/all_to_all | solution.py:90
  619.9 36.2 %copy.54 = f32[2,64,96,4,96]{2,3,4,1,0:T(4,128)} copy(f32[2,64,96,4,96]{2,1,0,4,3:T(8,128)S(1)} %bitcast.166) | data formatting | bytes 37748736 | tf_op jit(solution)/shard_map/all_to_all | solution.py:90
  656.2 26.3 %all_to_all.41 = f32[2,64,384,96]{2,3,1,0:T(8,128)} reshape(f32[2,64,4,96,96]{3,2,4,1,0:T(4,128)} %bitcast.167) | data formatting | bytes 37748736 | tf_op jit(solution)/shard_map/all_to_all | solution.py:90
  682.4 43.2 %convolution_bitcast_fusion.1 = f32[2,64,384,96]{2,3,1,0:T(8,128)S(1)} fusion(f32[2,64,384,96]{2,3,1,0:T(8,128)} %all_to_all.41, f32[384,384]{1,0:T(8,128)S(1)} %copy-done.2), kind=kOutput, calls=%fused_computation.80 | convolution fusion | flops 21743271936 | bytes 38338560 | tf_op jit(solution)/shard_map/ctjy,jb->ctby/dot_general | solution.py:91
  725.6 1.9 fusion.54
  727.5 2.1 fusion.53
  729.6 2.0 fusion.52
  731.6 2.0 fusion.51
  733.6 1.9 fusion.50
  735.6 2.1 fusion.49
  737.6 1.9 fusion.48
  739.6 2.0 fusion.47
  741.5 18.4 %copy.36 = f32[8,2,64,384,12]{3,2,4,1,0:T(8,128)} copy(f32[8,2,64,384,12]{3,4,2,1,0:T(8,128)} %fusion.47) | data formatting | bytes 37748736 | tf_op jit(solution)/shard_map/stack | solution.py:93
  760.0 9.2 all-to-all-start.1
  769.1 0.1 dynamic_slice.11
  769.2 0.1 broadcast_add_fusion
  769.4 408.5 %all-to-all-done.1 = f32[8,2,64,384,12]{3,2,4,1,0:T(8,128)} async-done(((f32[8,2,64,384,12]{3,2,4,1,0:T(8,128)}), f32[8,2,64,384,12]{3,2,4,1,0:T(8,128)}, u32[]{:S(2)}, u32[]{:S(2)}) %all-to-all-start.1) | async-done | bytes 18874400 | tf_op jit(solution)/shard_map/all_to_all | solution.py:93
  1177.8 12.8 copy.37
  1190.7 35.3 %convolution_bitcast_fusion = f32[2,512,384,12]{1,2,3,0:T(8,128)S(1)} fusion(f32[2,512,384,12]{2,1,3,0:T(8,128)} %bitcast.165, f32[512,512]{1,0:T(8,128)S(1)} %copy-done), kind=kOutput, calls=%fused_computation.79 | convolution fusion | flops 28991029248 | bytes 38797312 | tf_op jit(solution)/shard_map/cixy,ia->caxy/dot_general | solution.py:96
  1226.0 0.0 copy-start.1
  1226.0 6.5 copy-done.1
  1232.4 4.4 fusion.35
  1236.8 37.2 %all-reduce.3 = (f32[]{:T(128)}, f32[]{:T(128)}, f32[]{:T(128)}, f32[]{:T(128)}) all-reduce(f32[]{:T(128)} %get-tuple-element.5, f32[]{:T(128)} %get-tuple-element.24, f32[]{:T(128)} %get-tuple-element.4, f32[]{:T(128)} %get-tuple-element.3), channel_id=1, replica_groups=mesh['tm'=8,'space'=4] {'tm','space'}, use_global_device_ids=true, to_apply=%region_1.2 | all-reduce | flops 4 | bytes 32 | tf_op jit(solution)/shard_map/psum | solution.py:124
  1275.3 21.6 %fusion.44 = f32[1,512,384,12]{1,2,3,0:T(8,128)} fusion(f32[2,512,384,12]{1,2,3,0:T(8,128)} %copy-done.1, f32[]{:T(128)S(6)} %div.19, f32[12]{0:T(128)S(1)} %dynamic_slice.11, f32[512,384]{0,1:T(8,128)S(1)} %broadcast_add_fusion, f32[512,512]{1,0:T(8,128)S(1)} %copy-done), kind=kOutput, calls=%fused_computation.85 | convolution fusion | flops 14507311104 | bytes 30146612 | tf_op jit(solution)/shard_map/caxy,ia->cixy/dot_general | solution.py:100
  1296.9 23.1 %copy.39 = f32[1,512,384,12]{2,0,3,1:T(1,128)} copy(f32[1,512,384,12]{1,2,3,0:T(8,128)} %fusion.44) | data formatting | bytes 18874368 | tf_op jit(solution)/shard_map/caxy,ia->cixy/transpose | solution.py:100
  1320.0 210.6 %all_to_all.54 = f32[1,512,384,12]{2,0,3,1:T(1,128)S(1)} all-to-all(f32[1,512,384,12]{2,0,3,1:T(1,128)} %copy.39), channel_id=1, replica_groups=mesh['tm'=8,'space'=4] {'tm'}, dimensions={1} | all-to-all | bytes 18874368 | tf_op jit(solution)/shard_map/all_to_all | solution.py:101
  1530.6 4.6 copy.40
  1535.1 4.3 copy.41
  1539.5 24.3 %fusion.41 = f32[1,64,384,96]{2,3,1,0:T(8,128)} fusion(f32[64,384,96]{1,0,2:T(8,128)S(1)} %bitcast.169, f32[384,384]{1,0:T(8,128)S(1)} %copy-done.2), kind=kOutput, calls=%fused_computation.84 | convolution fusion | flops 10871635968 | bytes 19464192 | tf_op jit(solution)/shard_map/ctby,jb->ctjy/dot_general | solution.py:102
  1563.8 11.6 copy.43
  1575.4 6.6 all-to-all-start.3
  1584.5 12.0 multiply_subtract_fusion
  1596.5 12.0 multiply_add_fusion.4
  1608.5 111.5 %all-to-all-done.3 = f32[1,64,384,96]{3,1,0,2:T(8,128)} async-done(((f32[1,64,384,96]{3,1,0,2:T(8,128)}), f32[1,64,384,96]{3,1,0,2:T(8,128)}, u32[]{:S(2)}, u32[]{:S(2)}) %all-to-all-start.3) | async-done | bytes 9437216 | tf_op jit(solution)/shard_map/all_to_all | solution.py:103
  1719.9 16.4 copy.55
  1736.4 13.8 reshape.277
  1750.2 21.9 %multiply_add_fusion.3 = f32[64,96,384]{2,1,0:T(8,128)} fusion(f32[64,96,384]{2,1,0:T(8,128)} %param.12, f32[]{:T(128)S(6)} %div.23, f32[64,96,384]{2,1,0:T(8,128)} %reshape.277, f32[384,384]{1,0:T(8,128)S(1)} %copy-done.2), kind=kOutput, calls=%fused_computation.72 | convolution fusion | flops 10876354560 | bytes 28901380 | tf_op jit(solution)/shard_map/ctxa,ka->ctxk/dot_general | solution.py:104
  (10 shorter events, 0.1 us)
Async XLA Ops:
  0.6 1190.0 %copy-start = (f32[512,512]{1,0:T(8,128)S(1)}, f32[512,512]{1,0:T(8,128)}, u32[]{:S(2)}) copy-start(f32[512,512]{1,0:T(8,128)} %param.16) | copy-start | bytes 3145732
  1.9 5.7 collective-permute-start
  4.4 8.2 collective-permute-start.1
  7.6 10.7 copy-start.4
  7.7 10.9 copy-start.3
  12.8 11.6 collective-permute-start.2
  17.0 18.5 %collective-permute-start.3 = (f32[70,3,384]{2,1,0:T(4,128)S(1)}, f32[70,3,384]{2,1,0:T(4,128)S(1)}, u32[]{:S(2)}, u32[]{:S(2)}) collective-permute-start(f32[70,3,384]{2,1,0:T(4,128)S(1)} %get-tuple-element.29), channel_id=1, source_target_pairs={{1,0},{2,1},{3,2},{5,4},{6,5},{7,6},{9,8},{10,9},{11,10},{13,12},{... | collective-permute-start | bytes 967688 | tf_op jit(solution)/shard_map/ppermute | solution.py:19
  213.5 55.2 %copy-start.2 = (f32[384,384]{1,0:T(8,128)S(1)}, f32[384,384]{1,0:T(8,128)}, u32[]{:S(2)}) copy-start(f32[384,384]{1,0:T(8,128)} %param.17) | copy-start | bytes 1769476
  760.0 9.2 copy-start.5
  760.0 9.3 copy-start.6
  760.0 417.8 %all-to-all-start.1 = ((f32[8,2,64,384,12]{3,2,4,1,0:T(8,128)}), f32[8,2,64,384,12]{3,2,4,1,0:T(8,128)}, u32[]{:S(2)}, u32[]{:S(2)}) async-start(f32[8,2,64,384,12]{3,2,4,1,0:T(8,128)} %copy.36), calls=%async_computation.1 | async-start | bytes 37748736 | tf_op jit(solution)/shard_map/all_to_all | solution.py:93
  1226.0 6.5 copy-start.1
  1575.4 144.5 %all-to-all-start.3 = ((f32[1,64,384,96]{3,1,0,2:T(8,128)}), f32[1,64,384,96]{3,1,0,2:T(8,128)}, u32[]{:S(2)}, u32[]{:S(2)}) async-start(f32[1,64,384,96]{3,1,0,2:T(8,128)} %copy.43), calls=%async_computation.3 | async-start | bytes 25165824 | tf_op jit(solution)/shard_map/all_to_all | solution.py:103
